TPU v7x, 512 devices: a whole 4x4x16 slice. The times are simulated.
512 devices in a mesh: region: 128 (over z, x, core), pair: 4 (over y).
Axes of the slice: x: 4, y: 4, z: 16, core: 2. Of those that a mesh axis runs over, the one named last changes fastest.
Arguments:
- phi: bfloat16 [1024, 128, 32, 128], P('region', None, 'pair'), may hold values from -0.09375 to 0.09375
- potential: float32 [128, 32, 128], P('region', 'pair'), may hold values from -2 to 2
- pair_list: int32 [32, 2], replicated, may hold values from 0 to 7, as said below
- support: int32 [8, 128], replicated, may hold values 0 or 1
Outputs:
- intersection: float32 [32, 16384], P('pair', 'region')
- hamiltonian: float32 [32, 16384], P('pair', 'region')
- hphi: bfloat16 [1024, 128, 32, 128], P('region', None, 'pair')
Inputs may be any that keep to these rules, and one draw needn't show every extreme that they name: `pair_list`: each row is an ordered pair of block numbers; no pair appears twice.
All inputs are finite; a program needn't handle non-finite values.
Results may differ from a plain program's by a relative error of at most 0.0029.
Values may be sent and summed in bfloat16 or wider, within the bound.
No kernel may reach another device: no remote copies, remote signals or barrier semaphores. Data moves between devices by JAX's collectives and lax.ppermute only.
A program may use at most 64 MiB of HBM per device.

v0:
```python
import jax
import jax.numpy as jnp
from jax import lax
from jax.sharding import PartitionSpec as P

W = 128


def padded_2(block, sides, width):
    for axis, dim in sides:
        count = lax.axis_size(axis)
        forward = [(i, i + 1) for i in range(count - 1)]
        forward.append((count - 1, 0))
        backward = [(target, source) for source, target in forward]
        low = lax.ppermute(
            lax.slice_in_dim(block, block.shape[dim] - width, None, axis=dim), axis, forward
        )
        high = lax.ppermute(lax.slice_in_dim(block, 0, width, axis=dim), axis, backward)
        block = jnp.concatenate([low, block, high], axis=dim)
    return block


def apply_region(padded, potential, keep_value):
    values = padded.astype(jnp.float32)
    center = values[:, 1:-1, 1:-1]
    laplace_sum = values[:, 2:, 1:-1] + values[:, :-2, 1:-1] - 6.0 * center
    laplace_sum = laplace_sum + values[:, 1:-1, 2:] + values[:, 1:-1, :-2]
    z_padded = jnp.pad(center, ((0, 0), (0, 0), (0, 0), (1, 1)))
    laplace_sum = laplace_sum + z_padded[..., 2:] + z_padded[..., :-2]
    applied = (-0.5 * laplace_sum + potential[None] * center) * keep_value
    return applied.astype(jnp.bfloat16)


def local(phi, potential, pair_list, support):
    region_id = lax.axis_index("region")
    block_count = support.shape[0]
    all_funcs = block_count * W
    row_count = phi.shape[2]
    depth = phi.shape[3]
    plane_count = potential.shape[0]
    block_flags = lax.dynamic_slice_in_dim(support, region_id, 1, 1)[:, 0]
    func_live = jnp.repeat(block_flags > 0, W)
    region_data = lax.all_to_all(phi, "region", split_axis=1, concat_axis=0, tiled=True)
    confined = jnp.where(func_live[:, None, None, None], region_data, jnp.zeros_like(region_data))
    padded = padded_2(confined, (("region", 1), ("pair", 2)), 1)
    keep_values = block_flags.astype(jnp.float32)
    stacked = padded.reshape(block_count, W, plane_count + 2, row_count + 2, depth)
    applied_region = lax.map(
        lambda members: apply_region(members[0], potential, members[1]), (stacked, keep_values)
    )
    applied_region = applied_region.reshape(all_funcs, plane_count, row_count, depth)
    cell_count = plane_count * row_count * depth
    flat_data = confined.reshape(all_funcs, cell_count)
    flat_applied = applied_region.reshape(all_funcs, cell_count)
    contract_dims = (((1,), (1,)), ((), ()))

    def pair_terms(pair_row):
        left_rows = lax.dynamic_slice_in_dim(flat_data, pair_row[0] * W, W, 0)
        right_rows = lax.dynamic_slice_in_dim(flat_data, pair_row[1] * W, W, 0)
        ham_rows = lax.dynamic_slice_in_dim(flat_applied, pair_row[1] * W, W, 0)
        return (
            lax.dot_general(
                left_rows, right_rows, contract_dims, preferred_element_type=jnp.float32
            ),
            lax.dot_general(left_rows, ham_rows, contract_dims, preferred_element_type=jnp.float32),
        )

    intersection_part, hamil_part = lax.map(pair_terms, pair_list)
    pair_count = pair_list.shape[0]
    intersection_part = intersection_part.reshape(pair_count, W * W)
    hamil_part = hamil_part.reshape(pair_count, W * W)
    intersection_cols, hamil_cols = (
        lax.psum_scatter(intersection_part, "region", scatter_dimension=1, tiled=True),
        lax.psum_scatter(hamil_part, "region", scatter_dimension=1, tiled=True),
    )
    intersection, hamiltonian = (
        lax.psum_scatter(intersection_cols, "pair", scatter_dimension=0, tiled=True),
        lax.psum_scatter(hamil_cols, "pair", scatter_dimension=0, tiled=True),
    )
    hphi_out = lax.all_to_all(applied_region, "region", split_axis=0, concat_axis=1, tiled=True)
    return (intersection, hamiltonian, hphi_out)


def solution(mesh):
    in_specs = (P("region", None, "pair", None), P("region", "pair", None), P(), P())
    out_specs = (P("pair", "region"), P("pair", "region"), P("region", None, "pair", None))
    return jax.shard_map(local, mesh=mesh, in_specs=in_specs, out_specs=out_specs, check_vma=False)
```

profile of v0, /device:TPU:2, one launch (start us, length us, event | category | flops | bytes accessed | tf_op | source)
XLA Modules:
  0.0 986.6 jit_solution(11047298964091114942)
XLA Ops:
  7.2 3.5 copy.12
  10.7 19.6 %all-to-all-start = ((bf16[8,128,8,128]{3,2,0,1:T(8,128)(2,1)}), bf16[8,128,8,128]{3,2,0,1:T(8,128)(2,1)S(1)}, u32[]{:S(2)}, u32[]{:S(2)}) async-start(bf16[8,128,8,128]{3,2,0,1:T(8,128)(2,1)} %copy.12), calls=%async_computation | async-start | bytes 4194304 | tf_op jit(solution)/shard_map/all_to_all | solution.py:43
  30.5 96.1 %all-to-all-done = bf16[8,128,8,128]{3,2,0,1:T(8,128)(2,1)S(1)} async-done(((bf16[8,128,8,128]{3,2,0,1:T(8,128)(2,1)}), bf16[8,128,8,128]{3,2,0,1:T(8,128)(2,1)S(1)}, u32[]{:S(2)}, u32[]{:S(2)}) %all-to-all-start) | async-done | bytes 2097184 | tf_op jit(solution)/shard_map/all_to_all | solution.py:43
  126.6 3.7 bitcast_select_fusion.1
  130.3 2.7 collective-permute-start
  133.0 2.9 collective-permute-start.1
  135.9 21.8 %collective-permute-done = bf16[1024,1,8,128]{3,2,0,1:T(8,128)(2,1)S(1)} collective-permute-done((bf16[1024,1,8,128]{3,2,0,1:T(8,128)(2,1)S(1)}, bf16[1024,1,8,128]{3,2,0,1:T(8,128)(2,1)S(1)}, u32[]{:S(2)}, u32[]{:S(2)}) %collective-permute-start) | collective-permute-done | bytes 2097184 | tf_op jit(solution)/shard_map/ppermute | solution.py:15
  159.4 2.6 pad_maximum_fusion.3
  162.2 3.5 collective-permute-start.2
  166.7 3.6 collective-permute-start.3
  172.2 13.0 %collective-permute-done.2 = bf16[1024,3,1,128]{3,0,2,1:T(8,128)(2,1)} collective-permute-done((bf16[1024,3,1,128]{3,0,2,1:T(8,128)(2,1)S(1)}, bf16[1024,3,1,128]{3,0,2,1:T(8,128)(2,1)}, u32[]{:S(2)}, u32[]{:S(2)}) %collective-permute-start.2) | collective-permute-done | bytes 786464 | tf_op jit(solution)/shard_map/ppermute | solution.py:15
  185.2 2.3 copy.15
  189.1 2.3 copy.16
  191.5 10.7 %pad_maximum_fusion = bf16[1024,3,10,128]{3,2,0,1:T(8,128)(2,1)} fusion(bf16[1024,3,1,128]{3,2,0,1:T(2,128)(2,1)S(1)} %copy.16, bf16[1024,1,8,128]{3,2,0,1:T(8,128)(2,1)S(1)} %copy-done.7, bf16[1024,1,8,128]{3,2,0,1:T(8,128)(2,1)S(1)} %copy-done.1, bf16[1024,1,8,128]{3,2,0,1:T(8,128)(2,1)S(1)} %copy-done.5, bf16[1024,3,1,128]{3,2,0,1:T(2,128)(2,1)S(1)} %copy.15), kind=kLoop, calls=%fused_computation.25 | loop fusion | flops 39321600 | bytes 15728640 | tf_op jit(solution)/shard_map/concatenate | solution.py:19
  202.2 28.2 %while.24 = (s32[]{:T(128)}, bf16[8,128,1,8,128]{4,3,2,1,0:T(8,128)(2,1)S(1)}, bf16[8,128,3,10,128]{4,3,1,0,2:T(8,128)(2,1)}, f32[1,8,128]{2,1,0:T(8,128)S(1)}, f32[8]{0:T(128)S(1)}, /*index=5*/s32[]{:T(128)}) while((s32[]{:T(128)}, bf16[8,128,1,8,128]{4,3,2,1,0:T(8,128)(2,1)S(1)}, bf16[8,128,3,10,128]{4,3,1,0,2:T(8,128)(2,1)}, ...), condition=%wide.region_1.2_spmd, body=%wide.region_0.1_spmd.sunk | while | flops 2064386 | bytes 6885469 | solution.py:48
  230.4 2.0 copy.33
  232.3 10.9 %all-to-all-start.1 = ((bf16[1024,1,8,128]{3,2,1,0:T(8,128)(2,1)}), bf16[1024,1,8,128]{3,2,1,0:T(8,128)(2,1)S(1)}, u32[]{:S(2)}, u32[]{:S(2)}) async-start(bf16[1024,1,8,128]{3,2,1,0:T(8,128)(2,1)} %bitcast.76), calls=%async_computation.3 | async-start | bytes 4194304 | tf_op jit(solution)/shard_map/all_to_all | solution.py:80
  243.3 186.2 %while.25 = (s32[]{:T(128)}, f32[32,128,128]{2,1,0:T(8,128)}, f32[32,128,128]{2,1,0:T(8,128)}, s32[32,2]{0,1:T(2,128)S(1)}, bf16[1024,1024]{1,0:T(8,128)(2,1)}, ...) while((s32[]{:T(128)}, f32[32,128,128]{2,1,0:T(8,128)}, ...), condition=%wide.region_3.4_spmd, body=%wide.region_2.3_spmd.sunk | while | flops 67108872 | bytes 1180917 | solution.py:68
  251.2 1.9 fusion.29
  253.1 1.9 fusion.28
  257.0 1.9 fusion.29
  258.9 1.9 fusion.28
  262.8 1.9 fusion.29
  264.7 1.9 fusion.28
  268.6 1.9 fusion.29
  274.5 1.9 fusion.29
  280.3 1.9 fusion.29
  286.1 1.9 fusion.29
  291.9 1.9 fusion.29
  297.7 1.9 fusion.29
  299.6 1.9 fusion.28
  303.5 1.9 fusion.29
  305.4 1.9 fusion.28
  309.4 1.9 fusion.29
  315.2 1.9 fusion.29
  317.1 1.9 fusion.28
  326.9 1.9 fusion.29
  328.8 1.9 fusion.28
  338.5 1.9 fusion.29
  344.3 1.9 fusion.29
  346.2 1.9 fusion.28
  350.1 1.9 fusion.29
  352.0 1.9 fusion.28
  367.5 1.9 fusion.29
  369.4 1.9 fusion.28
  373.4 1.9 fusion.29
  379.2 1.9 fusion.29
  385.0 1.9 fusion.29
  386.9 1.9 fusion.28
  390.8 1.9 fusion.29
  392.7 1.9 fusion.28
  396.6 1.9 fusion.29
  402.5 1.9 fusion.29
  408.3 1.9 fusion.29
  414.1 1.9 fusion.29
  416.0 1.9 fusion.28
  419.9 1.9 fusion.29
  421.8 1.9 fusion.28
  425.7 1.9 fusion.29
  429.5 4.1 copy.32
  433.7 4.1 copy.31
  439.8 255.7 %reduce-scatter.3.cloned.1.call-done = f32[32,128]{1,0:T(8,128)} async-done(((f32[32,16384]{1,0:T(8,128)}), f32[32,128]{1,0:T(8,128)}) %reduce-scatter.3.cloned.1.call-update) | async-done | bytes 16400 | tf_op jit(solution)/shard_map/reduce_scatter | solution.py:73
  695.5 264.2 %reduce-scatter.5.cloned.1.call-done = f32[32,128]{1,0:T(8,128)} async-done(((f32[32,16384]{1,0:T(8,128)}), f32[32,128]{1,0:T(8,128)}) %reduce-scatter.5.cloned.1.call-update) | async-done | bytes 16400 | tf_op jit(solution)/shard_map/reduce_scatter | solution.py:74
  959.7 17.7 %all-reduce.3 = (f32[32,128]{1,0:T(8,128)S(1)}, f32[32,128]{1,0:T(8,128)S(1)}) all-reduce(f32[32,128]{1,0:T(8,128)} %reduce-scatter.3.cloned.1.call-done, f32[32,128]{1,0:T(8,128)} %reduce-scatter.5.cloned.1.call-done), channel_id=3, replica_groups=mesh['region'=128,'pair'=4] {'pair'}, use_global_device_ids=true, to_apply=%region_5.6.clone | all-reduce | flops 8192 | bytes 65536
  (160 shorter events, 103.3 us)
Async XLA Ops:
  10.7 19.6 %copy-start.10 = (s32[8,128]{1,0:T(8,128)S(1)}, s32[8,128]{1,0:T(8,128)}, u32[]{:S(2)}) copy-start(s32[8,128]{1,0:T(8,128)} %param.11) | copy-start | bytes 12292
  10.7 115.9 %all-to-all-start = ((bf16[8,128,8,128]{3,2,0,1:T(8,128)(2,1)}), bf16[8,128,8,128]{3,2,0,1:T(8,128)(2,1)S(1)}, u32[]{:S(2)}, u32[]{:S(2)}) async-start(bf16[8,128,8,128]{3,2,0,1:T(8,128)(2,1)} %copy.12), calls=%async_computation | async-start | bytes 4194304 | tf_op jit(solution)/shard_map/all_to_all | solution.py:43
  130.3 31.8 %copy-start = (bf16[1024,1,8,128]{3,2,0,1:T(8,128)(2,1)}, bf16[1024,1,8,128]{3,2,0,1:T(8,128)(2,1)S(1)}, u32[]{:S(2)}) copy-start(bf16[1024,1,8,128]{3,2,0,1:T(8,128)(2,1)S(1)} %bitcast_select_fusion.1) | copy-start | bytes 6291460
  130.3 27.4 %collective-permute-start = (bf16[1024,1,8,128]{3,2,0,1:T(8,128)(2,1)S(1)}, bf16[1024,1,8,128]{3,2,0,1:T(8,128)(2,1)S(1)}, u32[]{:S(2)}, u32[]{:S(2)}) collective-permute-start(bf16[1024,1,8,128]{3,2,0,1:T(8,128)(2,1)S(1)} %bitcast_select_fusion.1), channel_id=1, source_target_pairs={{0,4},{4,8},{8,12},{12,16},{16,20},{20,24},{24,28},{28,32},{32,36}... | collective-permute-start | bytes 6291464 | tf_op jit(solution)/shard_map/ppermute | solution.py:15
  133.0 26.4 %collective-permute-start.1 = (bf16[1024,1,8,128]{3,2,0,1:T(8,128)(2,1)S(1)}, bf16[1024,1,8,128]{3,2,0,1:T(8,128)(2,1)S(1)}, u32[]{:S(2)}, u32[]{:S(2)}) collective-permute-start(bf16[1024,1,8,128]{3,2,0,1:T(8,128)(2,1)S(1)} %bitcast_select_fusion.1), channel_id=1, source_target_pairs={{4,0},{8,4},{12,8},{16,12},{20,16},{24,20},{28,24},{32,28},{36,32}... | collective-permute-start | bytes 6291464 | tf_op jit(solution)/shard_map/ppermute | solution.py:18
  157.7 4.4 copy-start.4
  159.4 2.7 copy-start.6
  162.2 23.0 %collective-permute-start.2 = (bf16[1024,3,1,128]{3,0,2,1:T(8,128)(2,1)S(1)}, bf16[1024,3,1,128]{3,0,2,1:T(8,128)(2,1)}, u32[]{:S(2)}, u32[]{:S(2)}) collective-permute-start(bf16[1024,3,1,128]{3,0,2,1:T(8,128)(2,1)S(1)} %copy.13), channel_id=1, source_target_pairs={{0,1},{1,2},{2,3},{3,0},{4,5},{5,6},{6,7},{7,4},{8,9},{9,10},{10,1... | collective-permute-start | bytes 2359304 | tf_op jit(solution)/shard_map/ppermute | solution.py:15
  166.7 22.4 %collective-permute-start.3 = (bf16[1024,3,1,128]{3,0,2,1:T(8,128)(2,1)}, bf16[1024,3,1,128]{3,0,2,1:T(8,128)(2,1)}, u32[]{:S(2)}, u32[]{:S(2)}) collective-permute-start(bf16[1024,3,1,128]{3,0,2,1:T(8,128)(2,1)} %copy.14), channel_id=1, source_target_pairs={{1,0},{2,1},{3,2},{0,3},{5,4},{6,5},{7,6},{4,7},{9,8},{10,9},{11,1... | collective-permute-start | bytes 2359304 | tf_op jit(solution)/shard_map/ppermute | solution.py:18
  170.5 20.9 %copy-start.7 = (bf16[1024,1,8,128]{3,2,0,1:T(8,128)(2,1)S(1)}, bf16[1024,1,8,128]{3,2,0,1:T(8,128)(2,1)}, u32[]{:S(2)}) copy-start(bf16[1024,1,8,128]{3,2,0,1:T(8,128)(2,1)} %copy-done.6) | copy-start | bytes 6291460
  172.2 19.2 %copy-start.1 = (bf16[1024,1,8,128]{3,2,0,1:T(8,128)(2,1)S(1)}, bf16[1024,1,8,128]{3,2,0,1:T(8,128)(2,1)}, u32[]{:S(2)}) copy-start(bf16[1024,1,8,128]{3,2,0,1:T(8,128)(2,1)} %copy-done) | copy-start | bytes 6291460
  172.2 19.2 %copy-start.5 = (bf16[1024,1,8,128]{3,2,0,1:T(8,128)(2,1)S(1)}, bf16[1024,1,8,128]{3,2,0,1:T(8,128)(2,1)}, u32[]{:S(2)}) copy-start(bf16[1024,1,8,128]{3,2,0,1:T(8,128)(2,1)} %copy-done.4) | copy-start | bytes 6291460
  191.4 10.7 %copy-start.2 = (bf16[8,128,1,8,128]{4,3,2,1,0:T(8,128)(2,1)S(1)}, bf16[8,128,1,8,128]{4,3,2,1,0:T(8,128)(2,1)}, u32[]{:S(2)}) copy-start(bf16[8,128,1,8,128]{4,3,2,1,0:T(8,128)(2,1)} %custom-call) | copy-start | bytes 6291460
  191.4 10.7 %copy-start.8 = (f32[1,8,128]{2,1,0:T(8,128)S(1)}, f32[1,8,128]{2,1,0:T(8,128)}, u32[]{:S(2)}) copy-start(f32[1,8,128]{2,1,0:T(8,128)} %param.9) | copy-start | bytes 12292
  230.4 2.0 copy-start.3
  232.3 11.0 %copy-start.9 = (s32[32,2]{0,1:T(2,128)S(1)}, s32[32,2]{0,1:T(2,128)}, u32[]{:S(2)}) copy-start(s32[32,2]{0,1:T(2,128)} %param.10) | copy-start | bytes 772
  232.3 745.7 %all-to-all-start.1 = ((bf16[1024,1,8,128]{3,2,1,0:T(8,128)(2,1)}), bf16[1024,1,8,128]{3,2,1,0:T(8,128)(2,1)S(1)}, u32[]{:S(2)}, u32[]{:S(2)}) async-start(bf16[1024,1,8,128]{3,2,1,0:T(8,128)(2,1)} %bitcast.76), calls=%async_computation.3 | async-start | bytes 4194304 | tf_op jit(solution)/shard_map/all_to_all | solution.py:80
  243.3 452.2 %reduce-scatter.3.cloned.1.call-start = ((), (), s32[]{:S(2)}) async-start(), calls=%async_computation.4 | async-start | bytes 2113536 | tf_op jit(solution)/shard_map/reduce_scatter | solution.py:73
  433.7 526.0 %reduce-scatter.5.cloned.1.call-start = ((), (), s32[]{:S(2)}) async-start(), calls=%async_computation.5 | async-start | bytes 2113536 | tf_op jit(solution)/shard_map/reduce_scatter | solution.py:74
Sparse Core Ops, SparseCore 0:
  433.8 261.6 reduce-scatter.2
  700.7 259.0 reduce-scatter.4
where the time goes:
time: 989 us; the launch traced here: 987 us
  waiting for transfers between devices  654 us (66%)
  matrix products  121 us (12%)
  local copies, waits for them, and re-layouts  50.4 us (5%)
  loops' own time  43.5 us (4%)
  starting transfers between devices  43.2 us (4%)
  other arithmetic  41.4 us (4%)
  blocking collectives  17.7 us (2%)
  between operations  14.9 us (2%)
    reduce_scatter x1, waiting for transfers between devices, local(): lax.psum_scatter(hamil_part, 'region', scatter_dimension=1, tiled=True)  264 us
    reduce_scatter x1, waiting for transfers between devices, local(): lax.psum_scatter(intersection_part, 'region', scatter_dimension=1, tiled=...  256 us
    all_to_all x1, waiting for transfers between devices, local(): lax.all_to_all(phi, 'region', split_axis=1, concat_axis=0, tiled=True)  96.1 us
    dot_general x32, matrix products, pair_terms(): lax.dot_general(left_rows, ham_rows, contract_dims, preferred_element_typ...  60.8 us
    dot_general x32, matrix products, pair_terms(): lax.dot_general(left_rows, right_rows, contract_dims, preferred_element_t...  60.6 us
    another operation x1, loops' own time, local(): intersection_part, hamil_part = lax.map(pair_terms, pair_list)  43.2 us
    ppermute x2, waiting for transfers between devices, padded_2(): lax.ppermute(lax.slice_in_dim(block, block.shape[dim] - width, None, axis...  34.8 us
  transfers between devices with their start and end apart: 8, of which 7 were waited for; matrix products, arithmetic and copies ran while one was open for 16% of the time, Pallas kernels for 0%

commit v1 on v0

--- a/solution.py
+++ b/solution.py
@@ -40,7 +40,10 @@
     plane_count = potential.shape[0]
     block_flags = lax.dynamic_slice_in_dim(support, region_id, 1, 1)[:, 0]
     func_live = jnp.repeat(block_flags > 0, W)
-    region_data = lax.all_to_all(phi, "region", split_axis=1, concat_axis=0, tiled=True)
+    region_data = jnp.concatenate(
+        lax.all_to_all(jnp.stack(jnp.split(phi, lax.axis_size("region"), axis=1)), "region", 0, 0),
+        axis=0,
+    )
     confined = jnp.where(func_live[:, None, None, None], region_data, jnp.zeros_like(region_data))
     padded = padded_2(confined, (("region", 1), ("pair", 2)), 1)
     keep_values = block_flags.astype(jnp.float32)

time: 989 us -> 1140 us (1.15)
  local copies, waits for them, and re-layouts: 50.4 us -> 219 us
  other arithmetic: 41.4 us -> 23.6 us
    unnamed x29 -> x153, local copies, waits for them, and re-layouts: 17.4 us -> 182 us
  transfers between devices with their start and end apart: 8 -> 8, of which waited for: 7 -> 7; matrix products, arithmetic and copies ran while one was open for 16% -> 13% of each run, Pallas kernels for 0% -> 0%
where the time goes in v1:
time: 1140 us; the launch traced here: 1130 us
  waiting for transfers between devices  656 us (58%)
  local copies, waits for them, and re-layouts  219 us (19%)
  matrix products  121 us (11%)
  starting transfers between devices  43.2 us (4%)
  loops' own time  39.8 us (3%)
  other arithmetic  23.6 us (2%)
  blocking collectives  17.6 us (2%)
  between operations  14.9 us (1%)
    reduce_scatter x1, waiting for transfers between devices, local(): lax.psum_scatter(hamil_part, 'region', scatter_dimension=1, tiled=True)  264 us
    reduce_scatter x1, waiting for transfers between devices, local(): lax.psum_scatter(intersection_part, 'region', scatter_dimension=1, tiled=...  256 us
    unnamed x153, local copies, waits for them, and re-layouts  182 us
    all_to_all x1, waiting for transfers between devices, local(): lax.all_to_all(jnp.stack(jnp.split(phi, lax.axis_size('region'), axis=1))...  96.1 us
    dot_general x32, matrix products, pair_terms(): lax.dot_general(left_rows, right_rows, contract_dims, preferred_element_t...  60.6 us
    dot_general x32, matrix products, pair_terms(): lax.dot_general(left_rows, ham_rows, contract_dims, preferred_element_typ...  60.5 us
    another operation x1, loops' own time, local(): intersection_part, hamil_part = lax.map(pair_terms, pair_list)  39.5 us
    ppermute x2, waiting for transfers between devices, padded_2(): lax.ppermute(lax.slice_in_dim(block, block.shape[dim] - width, None, axis...  35.8 us
  transfers between devices with their start and end apart: 8, of which 7 were waited for; matrix products, arithmetic and copies ran while one was open for 13% of the time, Pallas kernels for 0%

profile of v1, /device:TPU:2, one launch (start us, length us, event | category | flops | bytes accessed | tf_op | source)
XLA Modules:
  0.0 1134.9 jit_solution(15765040174937163027)
XLA Ops:
  176.6 19.6 %all-to-all-start = ((bf16[128,8,1,8,128]{4,3,1,2,0:T(8,128)(2,1)}), bf16[128,8,1,8,128]{4,3,1,2,0:T(8,128)(2,1)S(1)}, u32[]{:S(2)}, u32[]{:S(2)}) async-start(bf16[128,8,1,8,128]{4,3,1,2,0:T(8,128)(2,1)} %constant_dynamic-update-slice_fusion), calls=%async_computation | async-start | bytes 4194304 | tf_op jit(solution)/shard_map/all_to_all | solution.py:44
  196.5 96.1 %all-to-all-done = bf16[128,8,1,8,128]{4,3,1,2,0:T(8,128)(2,1)S(1)} async-done(((bf16[128,8,1,8,128]{4,3,1,2,0:T(8,128)(2,1)}), bf16[128,8,1,8,128]{4,3,1,2,0:T(8,128)(2,1)S(1)}, u32[]{:S(2)}, u32[]{:S(2)}) %all-to-all-start) | async-done | bytes 2097184 | tf_op jit(solution)/shard_map/all_to_all | solution.py:44
  292.9 2.7 collective-permute-start
  295.6 2.9 collective-permute-start.1
  298.4 21.8 %collective-permute-done = bf16[1024,1,8,128]{3,0,2,1:T(8,128)(2,1)S(1)} collective-permute-done((bf16[1024,1,8,128]{3,0,2,1:T(8,128)(2,1)S(1)}, bf16[1024,1,8,128]{3,0,2,1:T(8,128)(2,1)S(1)}, u32[]{:S(2)}, u32[]{:S(2)}) %collective-permute-start) | collective-permute-done | bytes 2097184 | tf_op jit(solution)/shard_map/ppermute | solution.py:15
  323.8 3.5 collective-permute-start.2
  327.2 3.6 collective-permute-start.3
  332.8 14.0 %collective-permute-done.2 = bf16[1024,3,1,128]{3,0,2,1:T(8,128)(2,1)S(1)} collective-permute-done((bf16[1024,3,1,128]{3,0,2,1:T(8,128)(2,1)}, bf16[1024,3,1,128]{3,0,2,1:T(8,128)(2,1)S(1)}, u32[]{:S(2)}, u32[]{:S(2)}) %collective-permute-start.2) | collective-permute-done | bytes 786464 | tf_op jit(solution)/shard_map/ppermute | solution.py:15
  346.8 2.8 collective-permute-done.3
  349.6 5.9 pad_maximum_fusion
  355.5 30.0 %while.24 = (s32[]{:T(128)}, bf16[8,128,1,8,128]{4,3,2,1,0:T(8,128)(2,1)S(1)}, bf16[8,128,3,10,128]{4,1,0,3,2:T(8,128)(2,1)}, f32[1,8,128]{2,1,0:T(8,128)S(1)}, f32[8]{0:T(128)S(1)}, /*index=5*/s32[]{:T(128)}) while((s32[]{:T(128)}, bf16[8,128,1,8,128]{4,3,2,1,0:T(8,128)(2,1)S(1)}, bf16[8,128,3,10,128]{4,1,0,3,2:T(8,128)(2,1)}, ...), condition=%wide.region_1.2_spmd, body=%wide.region_0.1_spmd.sunk | while | flops 2064386 | bytes 8851549 | solution.py:51
  385.5 1.9 copy.536
  387.5 10.9 all-to-all-start.1
  398.5 179.7 %while.25 = (s32[]{:T(128)}, f32[32,128,128]{2,1,0:T(8,128)}, f32[32,128,128]{2,1,0:T(8,128)}, s32[32,2]{0,1:T(2,128)S(1)}, bf16[1024,1024]{1,0:T(8,128)(2,1)}, ...) while((s32[]{:T(128)}, f32[32,128,128]{2,1,0:T(8,128)}, ...), condition=%wide.region_3.4_spmd, body=%wide.region_2.3_spmd.sunk | while | flops 67108872 | bytes 1180917 | solution.py:71
  400.3 1.9 fusion.32
  402.2 1.9 fusion.31
  407.8 1.9 fusion.31
  411.6 1.9 fusion.32
  413.5 1.9 fusion.31
  417.2 1.9 fusion.32
  419.1 1.9 fusion.31
  424.7 1.9 fusion.31
  428.4 1.9 fusion.32
  430.3 1.9 fusion.31
  434.1 1.9 fusion.32
  436.0 1.9 fusion.31
  441.6 1.9 fusion.31
  445.3 1.9 fusion.32
  447.2 1.9 fusion.31
  452.8 1.9 fusion.31
  456.5 1.9 fusion.32
  458.4 1.9 fusion.31
  464.0 1.9 fusion.31
  469.6 1.9 fusion.31
  473.4 1.9 fusion.32
  475.3 1.9 fusion.31
  480.9 1.9 fusion.31
  486.5 1.9 fusion.31
  492.1 1.9 fusion.31
  497.7 1.9 fusion.31
  501.4 1.9 fusion.32
  503.3 1.9 fusion.31
  508.9 1.9 fusion.31
  512.7 1.9 fusion.32
  514.6 1.9 fusion.31
  520.2 1.9 fusion.31
  525.8 1.9 fusion.31
  531.4 1.9 fusion.31
  537.0 1.9 fusion.31
  540.7 1.9 fusion.32
  542.6 1.9 fusion.31
  548.2 1.9 fusion.31
  553.8 1.9 fusion.31
  557.6 1.9 fusion.32
  559.5 1.9 fusion.31
  565.1 1.9 fusion.31
  568.8 1.9 fusion.32
  570.7 1.9 fusion.31
  576.3 1.9 fusion.31
  578.2 4.1 copy.535
  582.4 4.1 copy.534
  588.5 255.5 %reduce-scatter.3.cloned.1.call-done = f32[32,128]{1,0:T(8,128)} async-done(((f32[32,16384]{1,0:T(8,128)}), f32[32,128]{1,0:T(8,128)}) %reduce-scatter.3.cloned.1.call-update) | async-done | bytes 16400 | tf_op jit(solution)/shard_map/reduce_scatter | solution.py:76
  844.0 264.2 %reduce-scatter.5.cloned.1.call-done = f32[32,128]{1,0:T(8,128)} async-done(((f32[32,16384]{1,0:T(8,128)}), f32[32,128]{1,0:T(8,128)}) %reduce-scatter.5.cloned.1.call-update) | async-done | bytes 16400 | tf_op jit(solution)/shard_map/reduce_scatter | solution.py:77
  1108.2 17.6 %all-reduce.3 = (f32[32,128]{1,0:T(8,128)S(1)}, f32[32,128]{1,0:T(8,128)S(1)}) all-reduce(f32[32,128]{1,0:T(8,128)} %reduce-scatter.3.cloned.1.call-done, f32[32,128]{1,0:T(8,128)} %reduce-scatter.5.cloned.1.call-done), channel_id=3, replica_groups=mesh['region'=128,'pair'=4] {'pair'}, use_global_device_ids=true, to_apply=%region_5.6.clone | all-reduce | flops 8192 | bytes 65536
  (289 shorter events, 263.9 us)
Async XLA Ops:
  176.6 19.6 %copy-start.9 = (s32[8,128]{1,0:T(8,128)S(1)}, s32[8,128]{1,0:T(8,128)}, u32[]{:S(2)}) copy-start(s32[8,128]{1,0:T(8,128)} %param.11) | copy-start | bytes 12292
  176.6 115.9 %all-to-all-start = ((bf16[128,8,1,8,128]{4,3,1,2,0:T(8,128)(2,1)}), bf16[128,8,1,8,128]{4,3,1,2,0:T(8,128)(2,1)S(1)}, u32[]{:S(2)}, u32[]{:S(2)}) async-start(bf16[128,8,1,8,128]{4,3,1,2,0:T(8,128)(2,1)} %constant_dynamic-update-slice_fusion), calls=%async_computation | async-start | bytes 4194304 | tf_op jit(solution)/shard_map/all_to_all | solution.py:44
  292.8 30.6 %copy-start = (bf16[1024,1,8,128]{3,0,2,1:T(8,128)(2,1)}, bf16[1024,1,8,128]{3,0,2,1:T(8,128)(2,1)S(1)}, u32[]{:S(2)}) copy-start(bf16[1024,1,8,128]{3,0,2,1:T(8,128)(2,1)S(1)} %bitcast_select_fusion.1) | copy-start | bytes 6291460
  292.9 27.4 %collective-permute-start = (bf16[1024,1,8,128]{3,0,2,1:T(8,128)(2,1)S(1)}, bf16[1024,1,8,128]{3,0,2,1:T(8,128)(2,1)S(1)}, u32[]{:S(2)}, u32[]{:S(2)}) collective-permute-start(bf16[1024,1,8,128]{3,0,2,1:T(8,128)(2,1)S(1)} %bitcast_select_fusion.1), channel_id=1, source_target_pairs={{0,4},{4,8},{8,12},{12,16},{16,20},{20,24},{24,28},{28,32},{32,36}... | collective-permute-start | bytes 6291464 | tf_op jit(solution)/shard_map/ppermute | solution.py:15
  295.6 26.4 %collective-permute-start.1 = (bf16[1024,1,8,128]{3,0,2,1:T(8,128)(2,1)S(1)}, bf16[1024,1,8,128]{3,0,2,1:T(8,128)(2,1)S(1)}, u32[]{:S(2)}, u32[]{:S(2)}) collective-permute-start(bf16[1024,1,8,128]{3,0,2,1:T(8,128)(2,1)S(1)} %bitcast_select_fusion.1), channel_id=1, source_target_pairs={{4,0},{8,4},{12,8},{16,12},{20,16},{24,20},{28,24},{32,28},{36,32}... | collective-permute-start | bytes 6291464 | tf_op jit(solution)/shard_map/ppermute | solution.py:18
  320.2 3.2 copy-start.2
  322.0 1.8 copy-start.4
  323.8 23.1 %collective-permute-start.2 = (bf16[1024,3,1,128]{3,0,2,1:T(8,128)(2,1)}, bf16[1024,3,1,128]{3,0,2,1:T(8,128)(2,1)S(1)}, u32[]{:S(2)}, u32[]{:S(2)}) collective-permute-start(bf16[1024,3,1,128]{3,0,2,1:T(8,128)(2,1)} %get-tuple-element.146), channel_id=1, source_target_pairs={{0,1},{1,2},{2,3},{3,0},{4,5},{5,6},{6,7},{7,4},{8,9},{9,10},{10,1... | collective-permute-start | bytes 2359304 | tf_op jit(solution)/shard_map/ppermute | solution.py:15
  327.2 22.4 %collective-permute-start.3 = (bf16[1024,3,1,128]{3,0,2,1:T(8,128)(2,1)}, bf16[1024,3,1,128]{3,0,2,1:T(8,128)(2,1)}, u32[]{:S(2)}, u32[]{:S(2)}) collective-permute-start(bf16[1024,3,1,128]{3,0,2,1:T(8,128)(2,1)} %get-tuple-element.147), channel_id=1, source_target_pairs={{1,0},{2,1},{3,2},{0,3},{5,4},{6,5},{7,6},{4,7},{9,8},{10,9},{11,1... | collective-permute-start | bytes 2359304 | tf_op jit(solution)/shard_map/ppermute | solution.py:18
  331.0 18.6 %copy-start.1 = (bf16[1024,1,8,128]{3,0,2,1:T(8,128)(2,1)S(1)}, bf16[1024,1,8,128]{3,0,2,1:T(8,128)(2,1)}, u32[]{:S(2)}) copy-start(bf16[1024,1,8,128]{3,0,2,1:T(8,128)(2,1)} %copy-done) | copy-start | bytes 6291460
  331.0 18.6 %copy-start.3 = (bf16[1024,1,8,128]{3,0,2,1:T(8,128)(2,1)S(1)}, bf16[1024,1,8,128]{3,0,2,1:T(8,128)(2,1)}, u32[]{:S(2)}) copy-start(bf16[1024,1,8,128]{3,0,2,1:T(8,128)(2,1)} %copy-done.2) | copy-start | bytes 6291460
  332.8 22.7 %copy-start.5 = (bf16[8,128,1,8,128]{4,3,2,1,0:T(8,128)(2,1)S(1)}, bf16[8,128,1,8,128]{4,3,2,1,0:T(8,128)(2,1)}, u32[]{:S(2)}) copy-start(bf16[8,128,1,8,128]{4,3,2,1,0:T(8,128)(2,1)} %custom-call.1) | copy-start | bytes 6291460
  332.8 22.7 %copy-start.7 = (f32[1,8,128]{2,1,0:T(8,128)S(1)}, f32[1,8,128]{2,1,0:T(8,128)}, u32[]{:S(2)}) copy-start(f32[1,8,128]{2,1,0:T(8,128)} %param.9) | copy-start | bytes 12292
  385.5 2.0 copy-start.6
  387.5 11.0 copy-start.8
  387.5 738.9 %all-to-all-start.1 = ((bf16[1024,1,8,128]{3,2,1,0:T(8,128)(2,1)}), bf16[1024,1,8,128]{3,2,1,0:T(8,128)(2,1)S(1)}, u32[]{:S(2)}, u32[]{:S(2)}) async-start(bf16[1024,1,8,128]{3,2,1,0:T(8,128)(2,1)} %bitcast.581), calls=%async_computation.3 | async-start | bytes 4194304 | tf_op jit(solution)/shard_map/all_to_all | solution.py:83
  398.4 445.5 %reduce-scatter.3.cloned.1.call-start = ((), (), s32[]{:S(2)}) async-start(), calls=%async_computation.4 | async-start | bytes 2113536 | tf_op jit(solution)/shard_map/reduce_scatter | solution.py:76
  582.3 525.8 %reduce-scatter.5.cloned.1.call-start = ((), (), s32[]{:S(2)}) async-start(), calls=%async_computation.5 | async-start | bytes 2113536 | tf_op jit(solution)/shard_map/reduce_scatter | solution.py:77
Sparse Core Ops, SparseCore 0:
  582.5 261.4 reduce-scatter.2
  849.2 258.9 reduce-scatter.4
